TPU v7x, 32 devices: a whole 2x2x4 slice. The times are simulated.
32 devices in a mesh: groups: 2 (over x), col: 16 (over z, y, core).
Axes of the slice: x: 2, y: 2, z: 4, core: 2. Of those that a mesh axis runs over, the one named last changes fastest.
Arguments:
- slab: float32 [2, 2048, 4096], P(None, 'groups', 'col'), parts along dimension 1, may hold values from -6 to 6
- block_on: int32 [16, 32], P('groups', 'col'), parts along dimension 0, may hold values 0 or 1
- block_band: int32 [16, 32], P('groups', 'col'), parts along dimension 0, may hold values from 0 to 3
- band_gain: float32 [4], replicated, may hold values from 0.25 to 2
Outputs:
- spectra: float32 [2, 2048, 4096], P(None, 'groups', 'col'), parts along dimension 1
There are 2 independent parts, one for each index of `groups`. A program takes and returns all parts, laid end to end along the dimension named above; an argument that names none is the same for every part. Nothing has to cross between parts.
All inputs are finite; a program needn't handle non-finite values. No bound on the sum of `block_on` on one device may be relied on, other than what follows from the above.
Results may differ from a plain program's by a relative error of at most 0.00007.
Values sent between devices are 32-bit elements; how exact they have to be, the bound alone decides.
No kernel may reach another device: no remote copies, remote signals or barrier semaphores. Data moves between devices by JAX's collectives and lax.ppermute only.
A program may use at most 64 MiB of HBM per device.

v0:
```python
import math
import jax
import jax.numpy as jnp
from jax import lax
from jax.sharding import PartitionSpec as P

BLOCK = 128


def phase_table(first_index, second_index, length):
    product = first_index[:, None] * second_index[None, :] % length
    angles = product.astype(jnp.float32) * (2.0 * math.pi / length)
    return (jnp.cos(angles), -jnp.sin(angles))


def contract(stacked, table, formula):
    cosine_table, sine_table = table
    real_part = jnp.einsum(
        formula, stacked[0], cosine_table, precision=lax.Precision.HIGHEST
    ) - jnp.einsum(formula, stacked[1], sine_table, precision=lax.Precision.HIGHEST)
    imag_part = jnp.einsum(
        formula, stacked[0], sine_table, precision=lax.Precision.HIGHEST
    ) + jnp.einsum(formula, stacked[1], cosine_table, precision=lax.Precision.HIGHEST)
    return jnp.stack([real_part, imag_part])


def rotate(stacked, table):
    cosine_table, sine_table = table
    real_part = stacked[0] * cosine_table - stacked[1] * sine_table
    imag_part = stacked[0] * sine_table + stacked[1] * cosine_table
    return jnp.stack([real_part, imag_part])


def shards(slab, block_on, block_band, band_gain):
    devices = lax.axis_size("col")
    rows_total = slab.shape[1]
    shard_cols = slab.shape[2]
    length = shard_cols * devices
    rows_here = rows_total // devices
    factor = 1.0 / math.sqrt(length)
    first_len = BLOCK
    second_len = length // first_len
    first_iota = jnp.arange(first_len, dtype=jnp.int32)
    second_iota = jnp.arange(second_len, dtype=jnp.int32)
    table_one = phase_table(first_iota, first_iota, first_len)
    table_middle = phase_table(first_iota, second_iota, length)
    table_two = phase_table(second_iota, second_iota, second_len)
    received = lax.all_to_all(
        slab.reshape(2, devices, rows_here, shard_cols),
        "col",
        split_axis=1,
        concat_axis=3,
        tiled=True,
    )
    row_count = received.shape[2]
    square = received[:, 0].reshape(2, row_count, first_len, second_len)
    mixture = contract(square, table_one, "rab,ak->rkb")
    mixture = rotate(mixture, table_middle)
    result = contract(mixture, table_two, "rkb,bm->rmk")
    whole = result.reshape(2, 1, row_count, length)
    whole = whole.reshape(2, rows_here, devices, shard_cols)
    spectrum = lax.all_to_all(whole, "col", split_axis=2, concat_axis=1, tiled=True).reshape(
        2, rows_total, shard_cols
    )
    choose = (block_band[..., None] == jnp.arange(band_gain.shape[0], dtype=jnp.int32)).astype(
        jnp.float32
    )
    weight = block_on.astype(jnp.float32) * jnp.sum(choose * band_gain, axis=-1) * factor
    row_blocks = rows_total // BLOCK
    col_blocks = shard_cols // BLOCK
    masked = (
        spectrum.reshape(2, row_blocks, BLOCK, col_blocks, BLOCK) * weight[None, :, None, :, None]
    )
    return masked.reshape(2, rows_total, shard_cols)


def solution(mesh):
    placed = (P(None, "groups", "col"), P("groups", "col"), P("groups", "col"), P())
    return jax.shard_map(
        shards, mesh=mesh, in_specs=placed, out_specs=P(None, "groups", "col"), check_vma=False
    )
```

profile of v0, /device:TPU:13, one launch (start us, length us, event | category | flops | bytes accessed | tf_op | source)
XLA Modules:
  0.0 138.4 jit_solution(2403043482625478237)
XLA Ops:
  0.0 3.1 %copy.54 = f32[2,16,64,256]{3,2,0,1:T(8,128)} copy(f32[2,16,64,256]{3,2,1,0:T(8,128)} %bitcast.56) | data formatting | bytes 4194304 | tf_op jit(solution)/shard_map/reshape | solution.py:49
  3.1 6.5 %all-to-all-start = ((f32[2,16,64,256]{3,2,0,1:T(8,128)}), f32[2,16,64,256]{3,2,0,1:T(8,128)S(1)}, u32[]{:S(2)}, u32[]{:S(2)}) async-start(f32[2,16,64,256]{3,2,0,1:T(8,128)} %copy.54), calls=%async_computation | async-start | bytes 4194304 | tf_op jit(solution)/shard_map/all_to_all | solution.py:48
  9.7 0.1 sine_negate_fusion.4
  9.7 47.3 %all-to-all-done = f32[2,16,64,256]{3,2,0,1:T(8,128)S(1)} async-done(((f32[2,16,64,256]{3,2,0,1:T(8,128)}), f32[2,16,64,256]{3,2,0,1:T(8,128)S(1)}, u32[]{:S(2)}, u32[]{:S(2)}) %all-to-all-start) | async-done | bytes 2097184 | tf_op jit(solution)/shard_map/all_to_all | solution.py:48
  57.1 1.2 fusion.79
  58.2 0.6 copy.55
  58.8 1.3 copy.56
  60.1 1.2 fusion.11
  61.4 2.2 %fusion.15 = f32[128,64,32]{0,1,2:T(8,128)} fusion(f32[64,128,32]{1,0,2:T(8,128)S(1)} %copy.56), kind=kOutput, calls=%fused_computation.27 | convolution fusion | flops 402882560 | bytes 2097152 | tf_op jit(solution)/shard_map/rab,ak->rkb/dot_general | solution.py:18
  63.6 1.9 %copy.57 = f32[1,1,64,16,256]{2,4,3,1,0:T(8,128)} copy(f32[1,1,64,16,256]{4,2,0,3,1:T(8,128)S(1)} %copy-done.1) | data formatting | bytes 2097152 | tf_op jit(solution)/shard_map/slice | solution.py:20
  65.5 2.7 %copy.58 = f32[64,128,32]{1,0,2:T(8,128)S(1)} copy(f32[64,128,32]{0,2,1:T(8,128)} %bitcast.52) | data formatting | bytes 2097152 | tf_op jit(solution)/shard_map/squeeze | solution.py:20
  68.2 0.0 copy-start
  68.2 1.3 convolution_add_fusion.1
  69.5 1.4 %add_bitcast_fusion = (f32[64,128,32]{1,0,2:T(8,128)S(1)}, f32[64,128,32]{1,0,2:T(8,128)S(1)}) fusion(f32[128,64,32]{0,1,2:T(8,128)S(1)} %convolution_add_fusion.1, f32[128,32]{0,1:T(8,128)S(1)} %get-tuple-element.9, f32[128,32]{0,1:T(8,128)S(1)} %get-tuple-element.10, f32[128,64,32]{0,1,2:T(8,128)S(1)} %copy-done, f32[64,128,32]{1,0,2:T(8,128)S(1)} %copy.58), kind=kOutput, calls=%fused_computation.9 | convolution fusion | flops 404733952 | bytes 5275648 | tf_op jit(solution)/shard_map/rab,ak->rkb/dot_general | solution.py:20
  70.9 1.6 %fusion.6 = f32[32,64,128]{2,0,1:T(8,128)S(1)} fusion(f32[64,128,32]{1,0,2:T(8,128)S(1)} %get-tuple-element.6), kind=kOutput, calls=%fused_computation.15 | convolution fusion | flops 100677632 | bytes 2097152 | tf_op jit(solution)/shard_map/rkb,bm->rmk/dot_general | solution.py:18
  72.5 1.6 %fusion.4 = f32[32,64,128]{2,0,1:T(8,128)S(1)} fusion(f32[64,128,32]{1,0,2:T(8,128)S(1)} %get-tuple-element.6), kind=kOutput, calls=%fused_computation.13 | convolution fusion | flops 100678656 | bytes 2097152 | tf_op jit(solution)/shard_map/rkb,bm->rmk/dot_general | solution.py:21
  74.1 1.8 %fusion.1 = f32[64,32,128]{2,1,0:T(8,128)S(1)} fusion(f32[32,64,128]{2,0,1:T(8,128)S(1)} %fusion.6, f32[64,128,32]{1,0,2:T(8,128)S(1)} %get-tuple-element.5), kind=kOutput, calls=%fused_computation.5 | convolution fusion | flops 100940800 | bytes 3145728 | tf_op jit(solution)/shard_map/rkb,bm->rmk/dot_general | solution.py:20
  75.9 1.3 stack.9
  77.1 2.8 %copy.65 = f32[1,64,16,256]{3,1,0,2:T(8,128)} copy(f32[1,64,16,256]{3,2,1,0:T(8,128)} %stack.9) | data formatting | bytes 2097152 | tf_op jit(solution)/shard_map/stack | solution.py:24
  79.9 1.6 %fusion = f32[64,32,128]{2,1,0:T(8,128)S(1)} fusion(f32[32,64,128]{2,0,1:T(8,128)S(1)} %fusion.4, f32[64,128,32]{1,0,2:T(8,128)S(1)} %get-tuple-element.5), kind=kOutput, calls=%fused_computation.3 | convolution fusion | flops 100939776 | bytes 3145728 | tf_op jit(solution)/shard_map/rkb,bm->rmk/dot_general | solution.py:23
  81.6 0.3 stack.10
  81.9 0.6 copy.66
  82.5 0.3 copy-done.2
  82.8 1.5 %pad_maximum_fusion = f32[2,64,16,256]{3,1,0,2:T(8,128)} fusion(f32[1,64,16,256]{3,1,0,2:T(8,128)S(1)} %copy.66, f32[1,64,16,256]{3,1,0,2:T(8,128)S(1)} %copy-done.2), kind=kLoop, calls=%fused_computation | loop fusion | flops 524288 | bytes 4194304 | tf_op jit(solution)/shard_map/stack | solution.py:24
  84.2 4.9 %all-to-all-start.1 = ((f32[2,64,16,256]{3,1,0,2:T(8,128)}), f32[2,64,16,256]{3,1,0,2:T(8,128)S(1)}, u32[]{:S(2)}, u32[]{:S(2)}) async-start(f32[2,64,16,256]{3,1,0,2:T(8,128)} %pad_maximum_fusion), calls=%async_computation.1 | async-start | bytes 4194304 | tf_op jit(solution)/shard_map/all_to_all | solution.py:62
  89.2 0.1 select_reduce_fusion
  89.3 0.1 copy.68
  89.4 0.3 mul.231
  89.7 0.1 copy.79
  89.8 46.8 %all-to-all-done.1 = f32[2,64,16,256]{3,1,0,2:T(8,128)S(1)} async-done(((f32[2,64,16,256]{3,1,0,2:T(8,128)}), f32[2,64,16,256]{3,1,0,2:T(8,128)S(1)}, u32[]{:S(2)}, u32[]{:S(2)}) %all-to-all-start.1) | async-done | bytes 2097184 | tf_op jit(solution)/shard_map/all_to_all | solution.py:62
  136.6 0.2 copy.67
  136.8 1.5 %bitcast_multiply_fusion = f32[2,1024,256]{2,1,0:T(8,128)} fusion(f32[2,64,16,256]{3,1,2,0:T(8,128)S(1)} %copy.67, f32[1024,256]{1,0:T(8,128)S(1)} %bitcast.54), kind=kLoop, calls=%fused_computation.1 | loop fusion | flops 524288 | bytes 5242880 | tf_op jit(solution)/shard_map/mul | solution.py:72
  (11 shorter events, 0.0 us)
Async XLA Ops:
  3.1 53.9 %all-to-all-start = ((f32[2,16,64,256]{3,2,0,1:T(8,128)}), f32[2,16,64,256]{3,2,0,1:T(8,128)S(1)}, u32[]{:S(2)}, u32[]{:S(2)}) async-start(f32[2,16,64,256]{3,2,0,1:T(8,128)} %copy.54), calls=%async_computation | async-start | bytes 4194304 | tf_op jit(solution)/shard_map/all_to_all | solution.py:48
  60.1 3.5 %copy-start.1 = (f32[1,1,64,16,256]{4,2,0,3,1:T(8,128)S(1)}, f32[1,1,64,16,256]{4,2,0,3,1:T(8,128)}, u32[]{:S(2)}) copy-start(f32[1,1,64,16,256]{4,2,0,3,1:T(8,128)} %get-tuple-element.7) | copy-start | bytes 3145732
  68.2 1.3 copy-start
  81.5 1.2 copy-start.2
  84.2 5.0 %copy-start.4 = (s32[8,2]{0,1:T(2,128)S(1)}, s32[8,2]{0,1:T(2,128)}, u32[]{:S(2)}) copy-start(s32[8,2]{0,1:T(2,128)} %param.6) | copy-start | bytes 196
  84.2 5.0 %copy-start.5 = (f32[4]{0:T(128)S(1)}, f32[4]{0:T(128)}, u32[]{:S(2)}) copy-start(f32[4]{0:T(128)} %param.7) | copy-start | bytes 52
  84.2 5.0 %copy-start.3 = (s32[8,2]{0,1:T(2,128)S(1)}, s32[8,2]{0,1:T(2,128)}, u32[]{:S(2)}) copy-start(s32[8,2]{0,1:T(2,128)} %param.5) | copy-start | bytes 196
  84.2 52.4 %all-to-all-start.1 = ((f32[2,64,16,256]{3,1,0,2:T(8,128)}), f32[2,64,16,256]{3,1,0,2:T(8,128)S(1)}, u32[]{:S(2)}, u32[]{:S(2)}) async-start(f32[2,64,16,256]{3,1,0,2:T(8,128)} %pad_maximum_fusion), calls=%async_computation.1 | async-start | bytes 4194304 | tf_op jit(solution)/shard_map/all_to_all | solution.py:62
where the time goes:
time: 139 us; the launch traced here: 138 us
  waiting for transfers between devices  94.1 us (68%)
  local copies, waits for them, and re-layouts  16.8 us (12%)
  matrix products  12.7 us (9%)
  starting transfers between devices  11.5 us (8%)
  other arithmetic  3.18 us (2%)
    all_to_all x1, waiting for transfers between devices, shards(): lax.all_to_all(slab.reshape(2, devices, rows_here, shard_cols), 'col', sp...  47.3 us
    all_to_all x1, waiting for transfers between devices, shards(): lax.all_to_all(whole, 'col', split_axis=2, concat_axis=1, tiled=True)  46.8 us
    all_to_all x1, starting transfers between devices, shards(): lax.all_to_all(slab.reshape(2, devices, rows_here, shard_cols), 'col', sp...  6.52 us
    another operation x4, local copies, waits for them, and re-layouts, contract(): return jnp.stack([real_part, imag_part])  4.98 us
    all_to_all x1, starting transfers between devices, shards(): lax.all_to_all(whole, 'col', split_axis=2, concat_axis=1, tiled=True)  4.94 us
    dot_general x2, matrix products, contract(): jnp.einsum(formula, stacked[0], cosine_table, precision=lax.Precision.HIG...  3.8 us
    dot_general x2, matrix products, contract(): jnp.einsum(formula, stacked[1], sine_table, precision=lax.Precision.HIGHEST)  3.18 us
    reshape x1, local copies, waits for them, and re-layouts, shards(): slab.reshape(2, devices, rows_here, shard_cols)  3.13 us
  transfers between devices with their start and end apart: 2, of which 2 were waited for; matrix products, arithmetic and copies ran while one was open for 0% of the time, Pallas kernels for 0%

commit v1 on v0

--- a/solution.py
+++ b/solution.py
@@ -5,6 +5,22 @@
 from jax.sharding import PartitionSpec as P
 
 BLOCK = 128
+
+
+def pairwise_exchange(x, axis, split, join):
+    ways, here = (lax.axis_size(axis), lax.axis_index(axis))
+    width = x.shape[split] // ways
+    shape = list(x.shape)
+    shape[split] = width
+    height = shape[join]
+    shape[join] = height * ways
+    full = jnp.zeros(shape, x.dtype)
+    for mask in range(ways):
+        part = lax.dynamic_slice_in_dim(x, (here ^ mask) * width, width, axis=split)
+        if mask:
+            part = lax.ppermute(part, axis, [(d, d ^ mask) for d in range(ways)])
+        full = lax.dynamic_update_slice_in_dim(full, part, (here ^ mask) * height, axis=join)
+    return full
 
 
 def phase_table(first_index, second_index, length):
@@ -59,9 +75,7 @@
     result = contract(mixture, table_two, "rkb,bm->rmk")
     whole = result.reshape(2, 1, row_count, length)
     whole = whole.reshape(2, rows_here, devices, shard_cols)
-    spectrum = lax.all_to_all(whole, "col", split_axis=2, concat_axis=1, tiled=True).reshape(
-        2, rows_total, shard_cols
-    )
+    spectrum = pairwise_exchange(whole, "col", 2, 1).reshape(2, rows_total, shard_cols)
     choose = (block_band[..., None] == jnp.arange(band_gain.shape[0], dtype=jnp.int32)).astype(
         jnp.float32
     )

time: 139 us -> 146 us (1.050)
  starting transfers between devices: 11.5 us -> 23 us
  waiting for transfers between devices: 94.1 us -> 85.9 us
  local copies, waits for them, and re-layouts: 16.8 us -> 19.1 us
  matrix products: 12.7 us -> 14.6 us
  other arithmetic: 3.18 us -> 1.7 us
    all_to_all x1 -> x0, waiting for transfers between devices: 46.8 us -> none  [shards(): lax.all_to_all(whole, 'col', split_axis=2, concat_axis=1, tiled=True)]
    ppermute x0 -> x15, waiting for transfers between devices: none -> 38.7 us  [pairwise_exchange(): part = lax.ppermute(part, axis, [(d, d ^ mask) for d in range(ways)])]
    ppermute x0 -> x15, starting transfers between devices: none -> 16.3 us  [pairwise_exchange(): part = lax.ppermute(part, axis, [(d, d ^ mask) for d in range(ways)])]
    all_to_all x1 -> x0, starting transfers between devices: 4.94 us -> none  [shards(): lax.all_to_all(whole, 'col', split_axis=2, concat_axis=1, tiled=True)]
    unnamed x13 -> x28, local copies, waits for them, and re-layouts: 0.39 us -> 2.05 us
    another operation x4 -> x3, local copies, waits for them, and re-layouts: 4.98 us -> 3.41 us  [contract(): return jnp.stack([real_part, imag_part])]
    another operation x1 -> x0, other arithmetic: 1.47 us -> none  [contract(): return jnp.stack([real_part, imag_part])]
  transfers between devices with their start and end apart: 2 -> 16, of which waited for: 2 -> 11; matrix products, arithmetic and copies ran while one was open for 0% -> 1% of each run, Pallas kernels for 0% -> 0%
where the time goes in v1:
time: 146 us; the launch traced here: 145 us
  waiting for transfers between devices  85.9 us (59%)
  starting transfers between devices  23 us (16%)
  local copies, waits for them, and re-layouts  19.1 us (13%)
  matrix products  14.6 us (10%)
  other arithmetic  1.7 us (1%)
    all_to_all x1, waiting for transfers between devices, shards(): lax.all_to_all(slab.reshape(2, devices, rows_here, shard_cols), 'col', sp...  47.2 us
    ppermute x15, waiting for transfers between devices, pairwise_exchange(): part = lax.ppermute(part, axis, [(d, d ^ mask) for d in range(ways)])  38.7 us
    ppermute x15, starting transfers between devices, pairwise_exchange(): part = lax.ppermute(part, axis, [(d, d ^ mask) for d in range(ways)])  16.3 us
    all_to_all x1, starting transfers between devices, shards(): lax.all_to_all(slab.reshape(2, devices, rows_here, shard_cols), 'col', sp...  6.65 us
    dot_general x2, matrix products, contract(): jnp.einsum(formula, stacked[1], cosine_table, precision=lax.Precision.HIG...  3.84 us
    dot_general x2, matrix products, contract(): jnp.einsum(formula, stacked[0], sine_table, precision=lax.Precision.HIGHEST)  3.82 us
    dot_general x2, matrix products, contract(): jnp.einsum(formula, stacked[0], cosine_table, precision=lax.Precision.HIG...  3.81 us
    another operation x3, local copies, waits for them, and re-layouts, contract(): return jnp.stack([real_part, imag_part])  3.41 us
  transfers between devices with their start and end apart: 16, of which 11 were waited for; matrix products, arithmetic and copies ran while one was open for 1% of the time, Pallas kernels for 0%

profile of v1, /device:TPU:13, one launch (start us, length us, event | category | flops | bytes accessed | tf_op | source)
XLA Modules:
  0.0 144.8 jit_solution(14577145780720802206)
XLA Ops:
  0.0 3.1 %copy.55 = f32[2,16,64,256]{3,2,0,1:T(8,128)} copy(f32[2,16,64,256]{3,2,1,0:T(8,128)} %bitcast.82) | data formatting | bytes 4194304 | tf_op jit(solution)/shard_map/reshape | solution.py:65
  3.1 6.7 %all-to-all-start = ((f32[2,16,64,256]{3,2,0,1:T(8,128)}), f32[2,16,64,256]{3,2,0,1:T(8,128)S(1)}, u32[]{:S(2)}, u32[]{:S(2)}) async-start(f32[2,16,64,256]{3,2,0,1:T(8,128)} %copy.55), calls=%async_computation | async-start | bytes 4194304 | tf_op jit(solution)/shard_map/all_to_all | solution.py:64
  10.0 47.2 %all-to-all-done = f32[2,16,64,256]{3,2,0,1:T(8,128)S(1)} async-done(((f32[2,16,64,256]{3,2,0,1:T(8,128)}), f32[2,16,64,256]{3,2,0,1:T(8,128)S(1)}, u32[]{:S(2)}, u32[]{:S(2)}) %all-to-all-start) | async-done | bytes 2097184 | tf_op jit(solution)/shard_map/all_to_all | solution.py:64
  59.0 1.3 copy.57
  60.3 1.2 fusion.11
  61.5 2.2 %fusion.15 = f32[128,64,32]{0,1,2:T(8,128)} fusion(f32[64,128,32]{1,0,2:T(8,128)S(1)} %copy.57), kind=kOutput, calls=%fused_computation.44 | convolution fusion | flops 402882560 | bytes 2097152 | tf_op jit(solution)/shard_map/rab,ak->rkb/dot_general | solution.py:34
  63.7 1.9 %copy.58 = f32[1,1,64,16,256]{2,4,3,1,0:T(8,128)} copy(f32[1,1,64,16,256]{4,2,0,3,1:T(8,128)S(1)} %copy-done.2) | data formatting | bytes 2097152 | tf_op jit(solution)/shard_map/slice | solution.py:36
  65.7 2.7 %copy.59 = f32[64,128,32]{1,0,2:T(8,128)S(1)} copy(f32[64,128,32]{0,2,1:T(8,128)} %bitcast.78) | data formatting | bytes 2097152 | tf_op jit(solution)/shard_map/squeeze | solution.py:36
  68.3 1.3 convolution_add_fusion.1
  69.6 1.4 add_bitcast_fusion
  71.0 1.6 %fusion.6 = f32[32,64,128]{2,0,1:T(8,128)S(1)} fusion(f32[64,128,32]{1,0,2:T(8,128)S(1)} %get-tuple-element.6), kind=kOutput, calls=%fused_computation.16 | convolution fusion | flops 100677632 | bytes 2097152 | tf_op jit(solution)/shard_map/rkb,bm->rmk/dot_general | solution.py:34
  72.7 2.6 %fusion.4 = f32[32,64,128]{2,0,1:T(8,128)} fusion(f32[64,128,32]{1,0,2:T(8,128)S(1)} %get-tuple-element.6), kind=kOutput, calls=%fused_computation.14 | convolution fusion | flops 100678656 | bytes 2097152 | tf_op jit(solution)/shard_map/rkb,bm->rmk/dot_general | solution.py:37
  75.2 1.8 %fusion.1 = f32[64,32,128]{2,1,0:T(8,128)S(1)} fusion(f32[32,64,128]{2,0,1:T(8,128)S(1)} %fusion.6, f32[64,128,32]{1,0,2:T(8,128)S(1)} %get-tuple-element.5), kind=kOutput, calls=%fused_computation.3 | convolution fusion | flops 100940800 | bytes 3145728 | tf_op jit(solution)/shard_map/rkb,bm->rmk/dot_general | solution.py:36
  77.0 1.3 stack.9
  78.3 1.9 %copy_dynamic-update-slice_fusion.1 = f32[2,64,16,256]{3,1,0,2:T(8,128)S(1)} fusion(f32[1,64,16,256]{3,2,1,0:T(8,128)} %stack.9), kind=kLoop, calls=%fused_computation.8 | loop fusion | bytes 2097152
  80.2 2.6 %fusion = f32[64,32,128]{2,1,0:T(8,128)} fusion(f32[32,64,128]{2,0,1:T(8,128)S(1)} %copy-done.1, f32[64,128,32]{1,0,2:T(8,128)S(1)} %get-tuple-element.5), kind=kOutput, calls=%fused_computation.1 | convolution fusion | flops 100939776 | bytes 3145728 | tf_op jit(solution)/shard_map/rkb,bm->rmk/dot_general | solution.py:39
  82.8 1.5 %stack.10 = f32[1,64,16,256]{3,2,1,0:T(8,128)S(1)} reshape(f32[64,32,128]{2,1,0:T(8,128)} %fusion) | data formatting | bytes 2097152 | tf_op jit(solution)/shard_map/stack | solution.py:40
  85.0 1.2 constant_dynamic-slice_fusion
  87.0 2.0 %collective-permute-start.2 = (f32[2,64,1,256]{3,1,0,2:T(8,128)}, f32[2,64,1,256]{3,1,0,2:T(8,128)S(1)}, u32[]{:S(2)}, u32[]{:S(2)}) collective-permute-start(f32[2,64,1,256]{3,1,0,2:T(8,128)} %get-tuple-element.19), channel_id=1, source_target_pairs={{0,3},{1,2},{2,1},{3,0},{4,7},{5,6},{6,5},{7,4},{8,11},{9,10},{10,... | collective-permute-start | bytes 393224 | tf_op jit(solution)/shard_map/ppermute | solution.py:21
  89.0 1.5 %collective-permute-start.4 = (f32[2,64,1,256]{3,1,0,2:T(8,128)}, f32[2,64,1,256]{3,1,0,2:T(8,128)S(1)}, u32[]{:S(2)}, u32[]{:S(2)}) collective-permute-start(f32[2,64,1,256]{3,1,0,2:T(8,128)} %get-tuple-element.17), channel_id=1, source_target_pairs={{0,5},{1,4},{2,7},{3,6},{4,1},{5,0},{6,3},{7,2},{8,13},{9,12},{10,... | collective-permute-start | bytes 393224 | tf_op jit(solution)/shard_map/ppermute | solution.py:21
  91.9 2.8 %collective-permute-start.6 = (f32[2,64,1,256]{3,1,0,2:T(8,128)S(1)}, f32[2,64,1,256]{3,1,0,2:T(8,128)S(1)}, u32[]{:S(2)}, u32[]{:S(2)}) collective-permute-start(f32[2,64,1,256]{3,1,0,2:T(8,128)S(1)} %copy-done.8), channel_id=1, source_target_pairs={{0,7},{1,6},{2,5},{3,4},{4,3},{5,2},{6,1},{7,0},{8,15},{9,14},{10,... | collective-permute-start | bytes 393224 | tf_op jit(solution)/shard_map/ppermute | solution.py:21
  97.7 1.2 collective-permute-start.9
  98.9 4.9 %collective-permute-done.5 = f32[2,64,1,256]{3,1,0,2:T(8,128)S(1)} collective-permute-done((f32[2,64,1,256]{3,1,0,2:T(8,128)S(1)}, f32[2,64,1,256]{3,1,0,2:T(8,128)S(1)}, u32[]{:S(2)}, u32[]{:S(2)}) %collective-permute-start.5) | collective-permute-done | bytes 131104 | tf_op jit(solution)/shard_map/ppermute | solution.py:21
  103.8 4.2 %collective-permute-start.10 = (f32[2,64,1,256]{3,1,0,2:T(8,128)S(1)}, f32[2,64,1,256]{3,1,0,2:T(8,128)S(1)}, u32[]{:S(2)}, u32[]{:S(2)}) collective-permute-start(f32[2,64,1,256]{3,1,0,2:T(8,128)S(1)} %copy-done.4), channel_id=1, source_target_pairs={{0,11},{1,10},{2,9},{3,8},{4,15},{5,14},{6,13},{7,12},{8,3},{9,2},... | collective-permute-start | bytes 393224 | tf_op jit(solution)/shard_map/ppermute | solution.py:21
  109.4 10.2 %collective-permute-done.8 = f32[2,64,1,256]{3,1,0,2:T(8,128)S(1)} collective-permute-done((f32[2,64,1,256]{3,1,0,2:T(8,128)S(1)}, f32[2,64,1,256]{3,1,0,2:T(8,128)S(1)}, u32[]{:S(2)}, u32[]{:S(2)}) %collective-permute-start.8) | collective-permute-done | bytes 131104 | tf_op jit(solution)/shard_map/ppermute | solution.py:21
  119.6 2.9 %collective-permute-done.9 = f32[2,64,1,256]{3,1,0,2:T(8,128)S(1)} collective-permute-done((f32[2,64,1,256]{3,1,0,2:T(8,128)S(1)}, f32[2,64,1,256]{3,1,0,2:T(8,128)S(1)}, u32[]{:S(2)}, u32[]{:S(2)}) %collective-permute-start.9) | collective-permute-done | bytes 131104 | tf_op jit(solution)/shard_map/ppermute | solution.py:21
  123.5 4.6 %collective-permute-done.10 = f32[2,64,1,256]{3,1,0,2:T(8,128)S(1)} collective-permute-done((f32[2,64,1,256]{3,1,0,2:T(8,128)S(1)}, f32[2,64,1,256]{3,1,0,2:T(8,128)S(1)}, u32[]{:S(2)}, u32[]{:S(2)}) %collective-permute-start.10) | collective-permute-done | bytes 131104 | tf_op jit(solution)/shard_map/ppermute | solution.py:21
  128.1 5.6 %collective-permute-done.11 = f32[2,64,1,256]{3,1,0,2:T(8,128)S(1)} collective-permute-done((f32[2,64,1,256]{3,1,0,2:T(8,128)S(1)}, f32[2,64,1,256]{3,1,0,2:T(8,128)S(1)}, u32[]{:S(2)}, u32[]{:S(2)}) %collective-permute-start.11) | collective-permute-done | bytes 131104 | tf_op jit(solution)/shard_map/ppermute | solution.py:21
  133.7 2.8 %collective-permute-done.12 = f32[2,64,1,256]{3,1,0,2:T(8,128)S(1)} collective-permute-done((f32[2,64,1,256]{3,1,0,2:T(8,128)S(1)}, f32[2,64,1,256]{3,1,0,2:T(8,128)S(1)}, u32[]{:S(2)}, u32[]{:S(2)}) %collective-permute-start.12) | collective-permute-done | bytes 131104 | tf_op jit(solution)/shard_map/ppermute | solution.py:21
  136.5 3.9 %collective-permute-done.13 = f32[2,64,1,256]{3,1,0,2:T(8,128)S(1)} collective-permute-done((f32[2,64,1,256]{3,1,0,2:T(8,128)S(1)}, f32[2,64,1,256]{3,1,0,2:T(8,128)S(1)}, u32[]{:S(2)}, u32[]{:S(2)}) %collective-permute-start.13) | collective-permute-done | bytes 131104 | tf_op jit(solution)/shard_map/ppermute | solution.py:21
  140.5 2.8 %collective-permute-done.14 = f32[2,64,1,256]{3,1,0,2:T(8,128)S(1)} collective-permute-done((f32[2,64,1,256]{3,1,0,2:T(8,128)S(1)}, f32[2,64,1,256]{3,1,0,2:T(8,128)S(1)}, u32[]{:S(2)}, u32[]{:S(2)}) %collective-permute-start.14) | collective-permute-done | bytes 131104 | tf_op jit(solution)/shard_map/ppermute | solution.py:21
  143.3 1.5 %broadcast_multiply_fusion = f32[2,1024,256]{2,1,0:T(8,128)} fusion(f32[2,1024,256]{2,1,0:T(8,128)S(1)} %bitcast_dynamic-update-slice_fusion, f32[1024,256]{1,0:T(8,128)S(1)} %bitcast.80), kind=kLoop, calls=%fused_computation.9 | loop fusion | flops 524288 | bytes 5242880 | tf_op jit(solution)/shard_map/mul | solution.py:86
  (69 shorter events, 10.1 us)
Async XLA Ops:
  3.1 6.7 %copy-start.11 = (s32[8,2]{0,1:T(2,128)S(1)}, s32[8,2]{0,1:T(2,128)}, u32[]{:S(2)}) copy-start(s32[8,2]{0,1:T(2,128)} %param.6) | copy-start | bytes 196
  3.1 6.8 %copy-start.12 = (f32[4]{0:T(128)S(1)}, f32[4]{0:T(128)}, u32[]{:S(2)}) copy-start(f32[4]{0:T(128)} %param.7) | copy-start | bytes 52
  3.1 54.1 %all-to-all-start = ((f32[2,16,64,256]{3,2,0,1:T(8,128)}), f32[2,16,64,256]{3,2,0,1:T(8,128)S(1)}, u32[]{:S(2)}, u32[]{:S(2)}) async-start(f32[2,16,64,256]{3,2,0,1:T(8,128)} %copy.55), calls=%async_computation | async-start | bytes 4194304 | tf_op jit(solution)/shard_map/all_to_all | solution.py:64
  60.3 3.5 %copy-start.2 = (f32[1,1,64,16,256]{4,2,0,3,1:T(8,128)S(1)}, f32[1,1,64,16,256]{4,2,0,3,1:T(8,128)}, u32[]{:S(2)}) copy-start(f32[1,1,64,16,256]{4,2,0,3,1:T(8,128)} %get-tuple-element.22) | copy-start | bytes 3145732
  68.3 1.3 copy-start
  78.3 1.9 %copy-start.1 = (f32[32,64,128]{2,0,1:T(8,128)S(1)}, f32[32,64,128]{2,0,1:T(8,128)}, u32[]{:S(2)}) copy-start(f32[32,64,128]{2,0,1:T(8,128)} %fusion.4) | copy-start | bytes 3145732
  84.9 1.3 copy-start.10
  86.1 4.5 %collective-permute-start = (f32[2,64,1,256]{3,1,0,2:T(8,128)}, f32[2,64,1,256]{3,1,0,2:T(8,128)}, u32[]{:S(2)}, u32[]{:S(2)}) collective-permute-start(f32[2,64,1,256]{3,1,0,2:T(8,128)} %get-tuple-element.21), channel_id=1, source_target_pairs={{0,1},{1,0},{2,3},{3,2},{4,5},{5,4},{6,7},{7,6},{8,9},{9,8},{10,11... | collective-permute-start | bytes 393224 | tf_op jit(solution)/shard_map/ppermute | solution.py:21
  86.9 3.8 %copy-start.9 = (f32[2,64,1,256]{3,1,0,2:T(8,128)S(1)}, f32[2,64,1,256]{3,1,0,2:T(8,128)}, u32[]{:S(2)}) copy-start(f32[2,64,1,256]{3,1,0,2:T(8,128)} %get-tuple-element.16) | copy-start | bytes 393220
  86.9 5.0 %copy-start.8 = (f32[2,64,1,256]{3,1,0,2:T(8,128)S(1)}, f32[2,64,1,256]{3,1,0,2:T(8,128)}, u32[]{:S(2)}) copy-start(f32[2,64,1,256]{3,1,0,2:T(8,128)} %get-tuple-element.15) | copy-start | bytes 393220
  86.9 8.7 %copy-start.7 = (f32[2,64,1,256]{3,1,0,2:T(8,128)S(1)}, f32[2,64,1,256]{3,1,0,2:T(8,128)}, u32[]{:S(2)}) copy-start(f32[2,64,1,256]{3,1,0,2:T(8,128)} %get-tuple-element.14) | copy-start | bytes 393220
  86.9 9.8 %copy-start.6 = (f32[2,64,1,256]{3,1,0,2:T(8,128)S(1)}, f32[2,64,1,256]{3,1,0,2:T(8,128)}, u32[]{:S(2)}) copy-start(f32[2,64,1,256]{3,1,0,2:T(8,128)} %get-tuple-element.13) | copy-start | bytes 393220
  86.9 10.8 %copy-start.5 = (f32[2,64,1,256]{3,1,0,2:T(8,128)S(1)}, f32[2,64,1,256]{3,1,0,2:T(8,128)}, u32[]{:S(2)}) copy-start(f32[2,64,1,256]{3,1,0,2:T(8,128)} %get-tuple-element.12) | copy-start | bytes 393220
  86.9 16.9 %copy-start.4 = (f32[2,64,1,256]{3,1,0,2:T(8,128)S(1)}, f32[2,64,1,256]{3,1,0,2:T(8,128)}, u32[]{:S(2)}) copy-start(f32[2,64,1,256]{3,1,0,2:T(8,128)} %get-tuple-element.11) | copy-start | bytes 393220
  86.9 21.1 %copy-start.3 = (f32[2,64,1,256]{3,1,0,2:T(8,128)S(1)}, f32[2,64,1,256]{3,1,0,2:T(8,128)}, u32[]{:S(2)}) copy-start(f32[2,64,1,256]{3,1,0,2:T(8,128)} %get-tuple-element.10) | copy-start | bytes 393220
  86.9 4.9 %collective-permute-start.1 = (f32[2,64,1,256]{3,1,0,2:T(8,128)}, f32[2,64,1,256]{3,1,0,2:T(8,128)S(1)}, u32[]{:S(2)}, u32[]{:S(2)}) collective-permute-start(f32[2,64,1,256]{3,1,0,2:T(8,128)} %get-tuple-element.20), channel_id=1, source_target_pairs={{0,2},{1,3},{2,0},{3,1},{4,6},{5,7},{6,4},{7,5},{8,10},{9,11},{10,... | collective-permute-start | bytes 393224 | tf_op jit(solution)/shard_map/ppermute | solution.py:21
  87.0 8.5 %collective-permute-start.2 = (f32[2,64,1,256]{3,1,0,2:T(8,128)}, f32[2,64,1,256]{3,1,0,2:T(8,128)S(1)}, u32[]{:S(2)}, u32[]{:S(2)}) collective-permute-start(f32[2,64,1,256]{3,1,0,2:T(8,128)} %get-tuple-element.19), channel_id=1, source_target_pairs={{0,3},{1,2},{2,1},{3,0},{4,7},{5,6},{6,5},{7,4},{8,11},{9,10},{10,... | collective-permute-start | bytes 393224 | tf_op jit(solution)/shard_map/ppermute | solution.py:21
  89.0 7.7 %collective-permute-start.3 = (f32[2,64,1,256]{3,1,0,2:T(8,128)}, f32[2,64,1,256]{3,1,0,2:T(8,128)S(1)}, u32[]{:S(2)}, u32[]{:S(2)}) collective-permute-start(f32[2,64,1,256]{3,1,0,2:T(8,128)} %get-tuple-element.18), channel_id=1, source_target_pairs={{0,4},{1,5},{2,6},{3,7},{4,0},{5,1},{6,2},{7,3},{8,12},{9,13},{10,... | collective-permute-start | bytes 393224 | tf_op jit(solution)/shard_map/ppermute | solution.py:21
  89.0 8.7 %collective-permute-start.4 = (f32[2,64,1,256]{3,1,0,2:T(8,128)}, f32[2,64,1,256]{3,1,0,2:T(8,128)S(1)}, u32[]{:S(2)}, u32[]{:S(2)}) collective-permute-start(f32[2,64,1,256]{3,1,0,2:T(8,128)} %get-tuple-element.17), channel_id=1, source_target_pairs={{0,5},{1,4},{2,7},{3,6},{4,1},{5,0},{6,3},{7,2},{8,13},{9,12},{10,... | collective-permute-start | bytes 393224 | tf_op jit(solution)/shard_map/ppermute | solution.py:21
  90.7 13.1 %collective-permute-start.5 = (f32[2,64,1,256]{3,1,0,2:T(8,128)S(1)}, f32[2,64,1,256]{3,1,0,2:T(8,128)S(1)}, u32[]{:S(2)}, u32[]{:S(2)}) collective-permute-start(f32[2,64,1,256]{3,1,0,2:T(8,128)S(1)} %copy-done.9), channel_id=1, source_target_pairs={{0,6},{1,7},{2,4},{3,5},{4,2},{5,3},{6,0},{7,1},{8,14},{9,15},{10,... | collective-permute-start | bytes 393224 | tf_op jit(solution)/shard_map/ppermute | solution.py:21
  91.9 16.2 %collective-permute-start.6 = (f32[2,64,1,256]{3,1,0,2:T(8,128)S(1)}, f32[2,64,1,256]{3,1,0,2:T(8,128)S(1)}, u32[]{:S(2)}, u32[]{:S(2)}) collective-permute-start(f32[2,64,1,256]{3,1,0,2:T(8,128)S(1)} %copy-done.8), channel_id=1, source_target_pairs={{0,7},{1,6},{2,5},{3,4},{4,3},{5,2},{6,1},{7,0},{8,15},{9,14},{10,... | collective-permute-start | bytes 393224 | tf_op jit(solution)/shard_map/ppermute | solution.py:21
  95.5 13.0 %collective-permute-start.7 = (f32[2,64,1,256]{3,1,0,2:T(8,128)S(1)}, f32[2,64,1,256]{3,1,0,2:T(8,128)S(1)}, u32[]{:S(2)}, u32[]{:S(2)}) collective-permute-start(f32[2,64,1,256]{3,1,0,2:T(8,128)S(1)} %copy-done.7), channel_id=1, source_target_pairs={{0,8},{1,9},{2,10},{3,11},{4,12},{5,13},{6,14},{7,15},{8,0},{9,1},... | collective-permute-start | bytes 393224 | tf_op jit(solution)/shard_map/ppermute | solution.py:21
  96.7 22.8 %collective-permute-start.8 = (f32[2,64,1,256]{3,1,0,2:T(8,128)S(1)}, f32[2,64,1,256]{3,1,0,2:T(8,128)S(1)}, u32[]{:S(2)}, u32[]{:S(2)}) collective-permute-start(f32[2,64,1,256]{3,1,0,2:T(8,128)S(1)} %copy-done.6), channel_id=1, source_target_pairs={{0,9},{1,8},{2,11},{3,10},{4,13},{5,12},{6,15},{7,14},{8,1},{9,0},... | collective-permute-start | bytes 393224 | tf_op jit(solution)/shard_map/ppermute | solution.py:21
  97.7 24.8 %collective-permute-start.9 = (f32[2,64,1,256]{3,1,0,2:T(8,128)S(1)}, f32[2,64,1,256]{3,1,0,2:T(8,128)S(1)}, u32[]{:S(2)}, u32[]{:S(2)}) collective-permute-start(f32[2,64,1,256]{3,1,0,2:T(8,128)S(1)} %copy-done.5), channel_id=1, source_target_pairs={{0,10},{1,11},{2,8},{3,9},{4,14},{5,15},{6,12},{7,13},{8,2},{9,3},... | collective-permute-start | bytes 393224 | tf_op jit(solution)/shard_map/ppermute | solution.py:21
  103.8 24.3 %collective-permute-start.10 = (f32[2,64,1,256]{3,1,0,2:T(8,128)S(1)}, f32[2,64,1,256]{3,1,0,2:T(8,128)S(1)}, u32[]{:S(2)}, u32[]{:S(2)}) collective-permute-start(f32[2,64,1,256]{3,1,0,2:T(8,128)S(1)} %copy-done.4), channel_id=1, source_target_pairs={{0,11},{1,10},{2,9},{3,8},{4,15},{5,14},{6,13},{7,12},{8,3},{9,2},... | collective-permute-start | bytes 393224 | tf_op jit(solution)/shard_map/ppermute | solution.py:21
  108.0 25.7 %collective-permute-start.11 = (f32[2,64,1,256]{3,1,0,2:T(8,128)S(1)}, f32[2,64,1,256]{3,1,0,2:T(8,128)S(1)}, u32[]{:S(2)}, u32[]{:S(2)}) collective-permute-start(f32[2,64,1,256]{3,1,0,2:T(8,128)S(1)} %copy-done.3), channel_id=1, source_target_pairs={{0,12},{1,13},{2,14},{3,15},{4,8},{5,9},{6,10},{7,11},{8,4},{9,5},... | collective-permute-start | bytes 393224 | tf_op jit(solution)/shard_map/ppermute | solution.py:21
  108.5 28.0 %collective-permute-start.12 = (f32[2,64,1,256]{3,1,0,2:T(8,128)S(1)}, f32[2,64,1,256]{3,1,0,2:T(8,128)S(1)}, u32[]{:S(2)}, u32[]{:S(2)}) collective-permute-start(f32[2,64,1,256]{3,1,0,2:T(8,128)S(1)} %get-tuple-element.9), channel_id=1, source_target_pairs={{0,13},{1,12},{2,15},{3,14},{4,9},{5,8},{6,11},{7,10},{8,5},{9,4},... | collective-permute-start | bytes 393224 | tf_op jit(solution)/shard_map/ppermute | solution.py:21
  119.5 20.9 %collective-permute-start.13 = (f32[2,64,1,256]{3,1,0,2:T(8,128)S(1)}, f32[2,64,1,256]{3,1,0,2:T(8,128)S(1)}, u32[]{:S(2)}, u32[]{:S(2)}) collective-permute-start(f32[2,64,1,256]{3,1,0,2:T(8,128)S(1)} %get-tuple-element.8), channel_id=1, source_target_pairs={{0,14},{1,15},{2,12},{3,13},{4,10},{5,11},{6,8},{7,9},{8,6},{9,7},... | collective-permute-start | bytes 393224 | tf_op jit(solution)/shard_map/ppermute | solution.py:21
  122.5 20.8 %collective-permute-start.14 = (f32[2,64,1,256]{3,1,0,2:T(8,128)S(1)}, f32[2,64,1,256]{3,1,0,2:T(8,128)S(1)}, u32[]{:S(2)}, u32[]{:S(2)}) collective-permute-start(f32[2,64,1,256]{3,1,0,2:T(8,128)S(1)} %get-tuple-element.7), channel_id=1, source_target_pairs={{0,15},{1,14},{2,13},{3,12},{4,11},{5,10},{6,9},{7,8},{8,7},{9,6},... | collective-permute-start | bytes 393224 | tf_op jit(solution)/shard_map/ppermute | solution.py:21
